TPU v7x, 32 devices: a whole 2x2x4 slice. The times are simulated.
32 devices in a mesh: row: 4 (over y, x), col: 8 (over z, core).
Axes of the slice: x: 2, y: 2, z: 4, core: 2. Of those that a mesh axis runs over, the one named last changes fastest.
Arguments:
- fact_block: int32 [98304, 1], P(('row', 'col')), may hold values from 0 to 31; in each aligned block of 3072 rows (0 to 3071, 3072 to 6143, ...) at most 192 rows name the same one
- fact_offset: int32 [98304], P(('row', 'col')), may hold values from 0 to 2047
- fact_date: int32 [98304], P(('row', 'col')), may hold values from 0 to 2555
- revenue: bfloat16 [98304], P(('row', 'col')), may hold values from 0.5 to 4
- supplier_words: int32 [2208], P('col'), may hold values from 0 to 1073741823
- date_words: int32 [88], P('col'), may hold values from 0 to 1073741823
- candidates: int32 [1024], replicated, may hold values from 0 to 65535
Outputs:
- supplier_revenue: float32 [65536], P(('row', 'col'))
- candidate_revenue: float32 [1024], replicated
- candidate_total: float32 [], replicated
Inputs may be any that keep to these rules, and one draw needn't show every extreme that they name: `fact_block`: each device's rows name no owner block more than 192 times. `candidates`: ids may repeat.
All inputs are finite; a program needn't handle non-finite values.
Results may differ from a plain program's by a relative error of at most 0.0003.
Values sent between devices are 32-bit elements; how exact they have to be, the bound alone decides.
A program may use at most 64 MiB of HBM per device.

v0:
```python
import jax
import jax.numpy as jnp
from jax import lax
from jax.sharding import PartitionSpec as P

SUP_DEV = 2048


def filtered_revenue(owner, fact_offset, fact_date, revenue, supplier_all, date_all):
    words_per_block = (SUP_DEV + 29) // 30
    word_index = owner * words_per_block + fact_offset // 30
    supplier_word = jnp.take(supplier_all, word_index)
    supplier_bit = jnp.bitwise_and(jnp.right_shift(supplier_word, fact_offset % 30), 1)
    date_slot = fact_date // 30
    positions = jnp.arange(date_all.shape[0], dtype=jnp.int32)
    date_word = jnp.sum(
        jnp.where(date_slot[:, None] == positions[None, :], date_all[None, :], 0), axis=1
    )
    date_bit = jnp.bitwise_and(jnp.right_shift(date_word, fact_date % 30), 1)
    return jnp.where(supplier_bit * date_bit == 1, revenue, jnp.zeros_like(revenue))


def per_device(fact_block, fact_offset, fact_date, revenue, supplier_words, date_words, candidates):
    devices = lax.axis_size("row") * lax.axis_size("col")
    supplier_all, date_all = (
        lax.all_gather(supplier_words, "col", axis=0, tiled=True),
        lax.all_gather(date_words, "col", axis=0, tiled=True),
    )
    owner = fact_block[:, 0]
    masked = filtered_revenue(owner, fact_offset, fact_date, revenue, supplier_all, date_all)
    row_count = fact_offset.shape[0]
    capacity = max(2, 2 * row_count // devices)
    row_ids = jnp.arange(row_count, dtype=jnp.int32)
    earlier = (owner[:, None] == owner[None, :]) & (row_ids[None, :] < row_ids[:, None])
    ranking = jnp.sum(earlier, axis=1, dtype=jnp.int32)
    slot_index = owner * capacity + ranking
    slot_revenue = (
        jnp.zeros((devices * capacity,), jnp.float32).at[slot_index].set(masked.astype(jnp.float32))
    )
    slot_offset = (
        jnp.zeros((devices * capacity,), jnp.float32)
        .at[slot_index]
        .set(fact_offset.astype(jnp.float32))
    )
    payload = jnp.stack((slot_revenue, slot_offset), axis=-1)
    payload = payload.reshape(lax.axis_size("row"), lax.axis_size("col"), 2 * capacity)
    arrived = lax.all_to_all(
        lax.all_to_all(payload, "row", split_axis=0, concat_axis=0, tiled=True),
        "col",
        split_axis=1,
        concat_axis=1,
        tiled=True,
    )
    arrived = arrived.reshape(-1, 2)
    owned = jax.ops.segment_sum(
        arrived[:, 0], arrived[:, 1].astype(jnp.int32), num_segments=SUP_DEV
    )
    global_id = owner * SUP_DEV + fact_offset
    onehot_cands = (global_id[:, None] == candidates[None, :]).astype(jnp.bfloat16)
    own_terms = jnp.dot(masked[None, :], onehot_cands, preferred_element_type=jnp.float32)[0]
    candidate_revenue = lax.psum(own_terms, ("row", "col"))
    candidate_total = jnp.sum(candidate_revenue)
    return (owned, candidate_revenue, candidate_total)


def solution(mesh):
    in_specs = (
        P(("row", "col"), None),
        P(("row", "col")),
        P(("row", "col")),
        P(("row", "col")),
        P("col"),
        P("col"),
        P(),
    )
    out_specs = (P(("row", "col")), P(), P())
    return jax.shard_map(
        per_device, mesh=mesh, in_specs=in_specs, out_specs=out_specs, check_vma=False
    )
```

profile of v0, /device:TPU:20, one launch (start us, length us, event | category | flops | bytes accessed | tf_op | source)
XLA Modules:
  0.0 186.4 jit_solution(15897103582751986480)
XLA Ops:
  0.6 1.2 dynamic-slice
  3.2 3.9 %convert_reduce_fusion = s32[3072]{0:T(1024)S(1)} fusion(s32[3072]{0:T(1024)} %bitcast.11), kind=kLoop, calls=%fused_computation.4 | loop fusion | flops 47182848 | bytes 24576 | tf_op jit(solution)/shard_map/reduce_sum | solution.py:35
  7.0 0.7 compare_select_fusion
  7.8 0.7 add_select_fusion.1
  8.5 0.8 multiply_add_fusion
  9.3 0.9 dynamic-update-slice.1
  10.2 0.9 dynamic-update-slice
  11.0 21.6 %all-reduce.2 = (s32[88]{0:T(128)S(1)}, s32[2208]{0:T(1024)S(1)}) all-reduce(s32[88]{0:T(128)S(1)} %dynamic-update-slice.1, s32[2208]{0:T(1024)S(1)} %dynamic-update-slice), channel_id=1, replica_groups=mesh['row'=4,'col'=8] {'col'}, use_global_device_ids=true, to_apply=%add.1 | all-reduce | flops 2296 | bytes 18368
  32.6 0.3 select_reduce_fusion
  32.9 0.0 copy-start
  32.9 0.0 copy-start.1
  32.9 0.0 copy-start.2
  32.9 0.0 copy-start.4
  32.9 17.4 %gather_fusion = s32[3072]{0:T(1024)S(1)} fusion(s32[2208]{0:T(1024)S(1)} %get-tuple-element.4, s32[3072]{0:T(1024)S(1)} %get-tuple-element.8), kind=kCustom, calls=%fused_computation | custom fusion | bytes 36864 | tf_op jit(solution)/shard_map/jit(_take)/gather | solution.py:12
  50.3 0.0 copy-done
  50.4 0.0 copy-done.1
  50.4 0.0 copy-done.2
  50.4 0.0 copy-done.4
  50.4 11.8 %scatter_custom_fusion = f32[6144]{0:T(1024)S(1)} fusion(s32[3072]{0:T(1024)S(1)} %bitcast.16, f32[3072]{0:T(1024)S(1)} %get-tuple-element.5, f32[]{:T(128)} %constant.30.clone.1), kind=kCustom, calls=%fused_computation.35 | custom fusion | bytes 24580 | tf_op jit(solution)/shard_map/scatter | solution.py:38
  62.2 11.8 %scatter_custom_fusion.1 = f32[6144]{0:T(1024)S(1)} fusion(s32[3072]{0:T(1024)S(1)} %bitcast.17, f32[3072]{0:T(1024)S(1)} %get-tuple-element.9, f32[]{:T(128)} %constant.30.clone.1), kind=kCustom, calls=%fused_computation.33 | custom fusion | bytes 24580 | tf_op jit(solution)/shard_map/scatter | solution.py:43
  74.1 0.0 copy-start.5
  74.1 1.1 copy.14
  75.2 2.7 %reshape.27 = f32[4,8,384]{2,1,0:T(8,128)} reshape(f32[6144,2]{1,0:T(8,128)S(1)} %copy.14) | data formatting | bytes 98304 | tf_op jit(solution)/shard_map/reshape | solution.py:46
  77.9 4.2 %all-to-all-start = ((f32[4,8,384]{2,1,0:T(8,128)}), f32[4,8,384]{2,1,0:T(8,128)S(1)}, u32[]{:S(2)}, u32[]{:S(2)}) async-start(f32[4,8,384]{2,1,0:T(8,128)} %reshape.27), calls=%async_computation | async-start | bytes 98304 | tf_op jit(solution)/shard_map/all_to_all | solution.py:48
  82.2 3.5 %all-to-all-done = f32[4,8,384]{2,1,0:T(8,128)S(1)} async-done(((f32[4,8,384]{2,1,0:T(8,128)}), f32[4,8,384]{2,1,0:T(8,128)S(1)}, u32[]{:S(2)}, u32[]{:S(2)}) %all-to-all-start) | async-done | bytes 49184 | tf_op jit(solution)/shard_map/all_to_all | solution.py:48
  85.7 0.6 copy.15
  86.3 10.8 %all-to-all-start.1 = ((f32[4,8,384]{2,0,1:T(4,128)}), f32[4,8,384]{2,0,1:T(4,128)S(1)}, u32[]{:S(2)}, u32[]{:S(2)}) async-start(f32[4,8,384]{2,0,1:T(4,128)} %copy.15), calls=%async_computation.1 | async-start | bytes 98304 | tf_op jit(solution)/shard_map/all_to_all | solution.py:47
  97.1 0.0 copy-done.5
  97.1 2.0 %fusion.1 = f32[1,1024]{1,0:T(1,128)S(1)} fusion(bf16[3072,1]{0,1:T(2,128)(2,1)S(1)} %reshape.72, s32[1024]{0:T(1024)S(1)} %copy-done.5, s32[3072]{0:T(1024)S(1)} %get-tuple-element.7), kind=kOutput, calls=%fused_computation.7 | convolution fusion | flops 9437184 | bytes 26624 | tf_op jit(solution)/shard_map/dot_general | solution.py:60
  99.1 40.9 %psum.7 = f32[1024]{0:T(1024)S(1)} all-reduce(f32[1024]{0:T(1024)S(1)} %bitcast.19), channel_id=1, replica_groups=mesh['row'=4,'col'=8] {'row','col'}, use_global_device_ids=true, to_apply=%region_5.6 | all-reduce | flops 1024 | bytes 8192 | tf_op jit(solution)/shard_map/psum | solution.py:61
  140.0 0.0 copy-start.3
  140.0 0.6 reduce_sum.32
  140.6 0.0 all-to-all-done.1
  140.6 3.2 %reshape.28 = f32[6144,2]{1,0:T(8,128)S(1)} reshape(f32[4,8,384]{2,1,0:T(8,128)S(1)} %copy.16) | data formatting | bytes 98304 | tf_op jit(solution)/shard_map/reshape | solution.py:54
  143.7 0.9 slice_reduce_fusion
  144.6 0.0 copy-done.3
  144.6 1.7 fusion.5
  146.3 40.0 %scatter_custom_fusion.2 = f32[2048]{0:T(1024)} fusion(s32[6144]{0:T(1024)S(1)} %fusion.5, f32[6144]{0:T(1024)S(1)} %slice_reduce_fusion, f32[]{:T(128)} %constant.30.clone.1), kind=kCustom, calls=%fused_computation.43 | custom fusion | flops 6144 | bytes 8196 | tf_op jit(solution)/shard_map/scatter-add | solution.py:55
  (6 shorter events, 0.1 us)
Async XLA Ops:
  32.9 17.5 %copy-start = (s32[3072,1]{0,1:T(1,128)S(1)}, s32[3072,1]{0,1:T(1,128)}, u32[]{:S(2)}) copy-start(s32[3072,1]{0,1:T(1,128)} %param.7) | copy-start | bytes 36868
  32.9 17.5 %copy-start.1 = (s32[3072]{0:T(1024)S(1)}, s32[3072]{0:T(1024)}, u32[]{:S(2)}) copy-start(s32[3072]{0:T(1024)} %param.9) | copy-start | bytes 36868
  32.9 17.5 %copy-start.2 = (s32[3072]{0:T(1024)S(1)}, s32[3072]{0:T(1024)}, u32[]{:S(2)}) copy-start(s32[3072]{0:T(1024)} %param.8) | copy-start | bytes 36868
  32.9 17.5 %copy-start.4 = (bf16[3072]{0:T(1024)(128)(2,1)S(1)}, bf16[3072]{0:T(1024)(128)(2,1)}, u32[]{:S(2)}) copy-start(bf16[3072]{0:T(1024)(128)(2,1)} %param.10) | copy-start | bytes 18436
  74.1 23.0 %copy-start.5 = (s32[1024]{0:T(1024)S(1)}, s32[1024]{0:T(1024)}, u32[]{:S(2)}) copy-start(s32[1024]{0:T(1024)} %param.13) | copy-start | bytes 12292
  77.9 7.7 %all-to-all-start = ((f32[4,8,384]{2,1,0:T(8,128)}), f32[4,8,384]{2,1,0:T(8,128)S(1)}, u32[]{:S(2)}, u32[]{:S(2)}) async-start(f32[4,8,384]{2,1,0:T(8,128)} %reshape.27), calls=%async_computation | async-start | bytes 98304 | tf_op jit(solution)/shard_map/all_to_all | solution.py:48
  86.3 54.3 %all-to-all-start.1 = ((f32[4,8,384]{2,0,1:T(4,128)}), f32[4,8,384]{2,0,1:T(4,128)S(1)}, u32[]{:S(2)}, u32[]{:S(2)}) async-start(f32[4,8,384]{2,0,1:T(4,128)} %copy.15), calls=%async_computation.1 | async-start | bytes 98304 | tf_op jit(solution)/shard_map/all_to_all | solution.py:47
  140.0 4.7 %copy-start.3 = (f32[1024]{0:T(1024)}, f32[1024]{0:T(1024)S(1)}, u32[]{:S(2)}) copy-start(f32[1024]{0:T(1024)S(1)} %psum.7) | copy-start | bytes 12292
where the time goes:
time: 187 us; the launch traced here: 186 us
  blocking collectives  62.5 us (33%)
  local copies, waits for them, and re-layouts  52.5 us (28%)
  other arithmetic  48.8 us (26%)
  starting transfers between devices  15 us (8%)
  waiting for transfers between devices  3.5 us (2%)
  between operations  2.1 us (1%)
  matrix products  2 us (1%)
    psum x1, blocking collectives, per_device(): candidate_revenue = lax.psum(own_terms, ('row', 'col'))  40.9 us
    scatter-add x1, other arithmetic, per_device(): jax.ops.segment_sum(arrived[:, 0], arrived[:, 1].astype(jnp.int32), num_s...  40 us
    unnamed x1, blocking collectives  21.6 us
    gather x1, local copies, waits for them, and re-layouts, filtered_revenue(): supplier_word = jnp.take(supplier_all, word_index)  17.4 us
    scatter x1, local copies, waits for them, and re-layouts, per_device(): slot_offset = jnp.zeros((devices * capacity,), jnp.float32).at[slot_index...  11.8 us
    scatter x1, local copies, waits for them, and re-layouts, per_device(): jnp.zeros((devices * capacity,), jnp.float32).at[slot_index]  11.8 us
    all_to_all x1, starting transfers between devices, per_device(): lax.all_to_all(lax.all_to_all(payload, 'row', split_axis=0, concat_axis=0...  10.8 us
    all_to_all x1, starting transfers between devices, per_device(): lax.all_to_all(payload, 'row', split_axis=0, concat_axis=0, tiled=True)  4.22 us
  transfers between devices with their start and end apart: 2, of which 1 were waited for; matrix products, arithmetic and copies ran while one was open for 1% of the time, Pallas kernels for 0%

commit v1 on v0

--- a/solution.py
+++ b/solution.py
@@ -2,6 +2,7 @@
 import jax.numpy as jnp
 from jax import lax
 from jax.sharding import PartitionSpec as P
+from jax.lax import psum
 
 SUP_DEV = 2048
 
@@ -58,7 +59,8 @@
     global_id = owner * SUP_DEV + fact_offset
     onehot_cands = (global_id[:, None] == candidates[None, :]).astype(jnp.bfloat16)
     own_terms = jnp.dot(masked[None, :], onehot_cands, preferred_element_type=jnp.float32)[0]
-    candidate_revenue = lax.psum(own_terms, ("row", "col"))
+    trace_the_thing = lambda target: psum(psum(target, "col"), "row")
+    candidate_revenue = trace_the_thing(own_terms)
     candidate_total = jnp.sum(candidate_revenue)
     return (owned, candidate_revenue, candidate_total)
 

time: 187 us -> 172 us (0.920)
  the two profiles are of different devices: /device:TPU:20 before, /device:TPU:4 now
where the time goes in v1:
time: 172 us; the launch traced here: 171 us
  blocking collectives  54.8 us (32%)
  local copies, waits for them, and re-layouts  52.5 us (31%)
  other arithmetic  48.2 us (28%)
  starting transfers between devices  7.56 us (4%)
  waiting for transfers between devices  3.46 us (2%)
  between operations  2.12 us (1%)
  matrix products  2.01 us (1%)
    scatter-add x1, other arithmetic, per_device(): jax.ops.segment_sum(arrived[:, 0], arrived[:, 1].astype(jnp.int32), num_s...  39.4 us
    unnamed x1, blocking collectives  28.8 us
    psum x2, blocking collectives, per_device(): trace_the_thing = lambda target: psum(psum(target, 'col'), 'row')  26 us
    gather x1, local copies, waits for them, and re-layouts, filtered_revenue(): supplier_word = jnp.take(supplier_all, word_index)  17.4 us
    scatter x1, local copies, waits for them, and re-layouts, per_device(): jnp.zeros((devices * capacity,), jnp.float32).at[slot_index]  11.8 us
    scatter x1, local copies, waits for them, and re-layouts, per_device(): slot_offset = jnp.zeros((devices * capacity,), jnp.float32).at[slot_index...  11.8 us
    all_to_all x1, starting transfers between devices, per_device(): lax.all_to_all(payload, 'row', split_axis=0, concat_axis=0, tiled=True)  4.22 us
    reduce_sum x1, other arithmetic, per_device(): ranking = jnp.sum(earlier, axis=1, dtype=jnp.int32)  3.86 us
  transfers between devices with their start and end apart: 2, of which 1 were waited for; matrix products, arithmetic and copies ran while one was open for 2% of the time, Pallas kernels for 0%

profile of v1, /device:TPU:4, one launch (start us, length us, event | category | flops | bytes accessed | tf_op | source)
XLA Modules:
  0.0 170.6 jit_solution(9906170093563342530)
XLA Ops:
  0.6 1.2 dynamic-slice
  3.2 3.9 %convert_reduce_fusion = s32[3072]{0:T(1024)S(1)} fusion(s32[3072]{0:T(1024)} %bitcast.11), kind=kLoop, calls=%fused_computation.4 | loop fusion | flops 47182848 | bytes 24576 | tf_op jit(solution)/shard_map/reduce_sum | solution.py:36
  7.0 0.7 compare_select_fusion
  7.8 0.7 add_select_fusion.1
  8.5 0.8 multiply_add_fusion
  9.3 0.9 dynamic-update-slice.1
  10.2 0.9 dynamic-update-slice
  11.0 28.8 %all-reduce.2 = (s32[88]{0:T(128)S(1)}, s32[2208]{0:T(1024)S(1)}) all-reduce(s32[88]{0:T(128)S(1)} %dynamic-update-slice.1, s32[2208]{0:T(1024)S(1)} %dynamic-update-slice), channel_id=1, replica_groups=mesh['row'=4,'col'=8] {'col'}, use_global_device_ids=true, to_apply=%add.1 | all-reduce | flops 2296 | bytes 18368
  39.8 0.3 select_reduce_fusion
  40.1 0.0 copy-start
  40.1 0.0 copy-start.1
  40.1 0.0 copy-start.2
  40.1 0.0 copy-start.4
  40.1 17.4 %gather_fusion = s32[3072]{0:T(1024)S(1)} fusion(s32[2208]{0:T(1024)S(1)} %get-tuple-element.4, s32[3072]{0:T(1024)S(1)} %get-tuple-element.8), kind=kCustom, calls=%fused_computation | custom fusion | bytes 36864 | tf_op jit(solution)/shard_map/jit(_take)/gather | solution.py:13
  57.6 0.0 copy-done
  57.6 0.0 copy-done.1
  57.6 0.0 copy-done.2
  57.6 0.0 copy-done.4
  57.6 11.8 %scatter_custom_fusion = f32[6144]{0:T(1024)S(1)} fusion(s32[3072]{0:T(1024)S(1)} %bitcast.16, f32[3072]{0:T(1024)S(1)} %get-tuple-element.5, f32[]{:T(128)} %constant.30.clone.1), kind=kCustom, calls=%fused_computation.35 | custom fusion | bytes 24580 | tf_op jit(solution)/shard_map/scatter | solution.py:39
  69.5 11.8 %scatter_custom_fusion.1 = f32[6144]{0:T(1024)S(1)} fusion(s32[3072]{0:T(1024)S(1)} %bitcast.17, f32[3072]{0:T(1024)S(1)} %get-tuple-element.9, f32[]{:T(128)} %constant.30.clone.1), kind=kCustom, calls=%fused_computation.33 | custom fusion | bytes 24580 | tf_op jit(solution)/shard_map/scatter | solution.py:44
  81.3 0.0 copy-start.5
  81.3 1.1 copy.14
  82.4 2.7 %reshape.27 = f32[4,8,384]{2,1,0:T(8,128)} reshape(f32[6144,2]{1,0:T(8,128)S(1)} %copy.14) | data formatting | bytes 98304 | tf_op jit(solution)/shard_map/reshape | solution.py:47
  85.1 4.2 %all-to-all-start = ((f32[4,8,384]{2,1,0:T(8,128)}), f32[4,8,384]{2,1,0:T(8,128)S(1)}, u32[]{:S(2)}, u32[]{:S(2)}) async-start(f32[4,8,384]{2,1,0:T(8,128)} %reshape.27), calls=%async_computation | async-start | bytes 98304 | tf_op jit(solution)/shard_map/all_to_all | solution.py:49
  89.4 3.5 %all-to-all-done = f32[4,8,384]{2,1,0:T(8,128)S(1)} async-done(((f32[4,8,384]{2,1,0:T(8,128)}), f32[4,8,384]{2,1,0:T(8,128)S(1)}, u32[]{:S(2)}, u32[]{:S(2)}) %all-to-all-start) | async-done | bytes 49184 | tf_op jit(solution)/shard_map/all_to_all | solution.py:49
  92.8 0.6 copy.15
  93.5 3.3 %all-to-all-start.1 = ((f32[4,8,384]{2,0,1:T(4,128)}), f32[4,8,384]{2,0,1:T(4,128)S(1)}, u32[]{:S(2)}, u32[]{:S(2)}) async-start(f32[4,8,384]{2,0,1:T(4,128)} %copy.15), calls=%async_computation.1 | async-start | bytes 98304 | tf_op jit(solution)/shard_map/all_to_all | solution.py:48
  96.8 0.0 copy-done.5
  96.8 2.0 %fusion.1 = f32[1,1024]{1,0:T(1,128)S(1)} fusion(bf16[3072,1]{0,1:T(2,128)(2,1)S(1)} %reshape.72, s32[1024]{0:T(1024)S(1)} %copy-done.5, s32[3072]{0:T(1024)S(1)} %get-tuple-element.7), kind=kOutput, calls=%fused_computation.7 | convolution fusion | flops 9437184 | bytes 26624 | tf_op jit(solution)/shard_map/dot_general | solution.py:61
  98.8 17.0 %psum.14 = f32[1024]{0:T(1024)S(1)} all-reduce(f32[1024]{0:T(1024)S(1)} %bitcast.19), channel_id=1, replica_groups=mesh['row'=4,'col'=8] {'col'}, use_global_device_ids=true, to_apply=%region_5.6 | all-reduce | flops 1024 | bytes 8192 | tf_op jit(solution)/shard_map/psum | solution.py:62
  115.9 8.9 %psum.15 = f32[1024]{0:T(1024)S(1)} all-reduce(f32[1024]{0:T(1024)S(1)} %psum.14), channel_id=1, replica_groups=mesh['row'=4,'col'=8] {'row'}, use_global_device_ids=true, to_apply=%region_6.7 | all-reduce | flops 1024 | bytes 8192 | tf_op jit(solution)/shard_map/psum | solution.py:62
  124.8 0.0 copy-start.3
  124.8 0.6 reduce_sum.32
  125.4 0.0 all-to-all-done.1
  125.4 3.2 %reshape.28 = f32[6144,2]{1,0:T(8,128)S(1)} reshape(f32[4,8,384]{2,1,0:T(8,128)S(1)} %copy.16) | data formatting | bytes 98304 | tf_op jit(solution)/shard_map/reshape | solution.py:55
  128.6 0.9 slice_reduce_fusion
  129.5 0.0 copy-done.3
  129.5 1.7 %fusion.5 = s32[6144]{0:T(1024)S(1)} fusion(f32[6144,2]{1,0:T(8,128)S(1)} %reshape.28), kind=kLoop, calls=%fused_computation.13 | loop fusion | flops 6144 | bytes 49152 | tf_op jit(solution)/shard_map/convert_element_type | solution.py:57
  131.2 39.4 %scatter_custom_fusion.2 = f32[2048]{0:T(1024)} fusion(s32[6144]{0:T(1024)S(1)} %fusion.5, f32[6144]{0:T(1024)S(1)} %slice_reduce_fusion, f32[]{:T(128)} %constant.30.clone.1), kind=kCustom, calls=%fused_computation.43 | custom fusion | flops 6144 | bytes 8196 | tf_op jit(solution)/shard_map/scatter-add | solution.py:56
  (6 shorter events, 0.1 us)
Async XLA Ops:
  40.1 17.5 %copy-start = (s32[3072,1]{0,1:T(1,128)S(1)}, s32[3072,1]{0,1:T(1,128)}, u32[]{:S(2)}) copy-start(s32[3072,1]{0,1:T(1,128)} %param.7) | copy-start | bytes 36868
  40.1 17.5 %copy-start.1 = (s32[3072]{0:T(1024)S(1)}, s32[3072]{0:T(1024)}, u32[]{:S(2)}) copy-start(s32[3072]{0:T(1024)} %param.9) | copy-start | bytes 36868
  40.1 17.5 %copy-start.2 = (s32[3072]{0:T(1024)S(1)}, s32[3072]{0:T(1024)}, u32[]{:S(2)}) copy-start(s32[3072]{0:T(1024)} %param.8) | copy-start | bytes 36868
  40.1 17.5 %copy-start.4 = (bf16[3072]{0:T(1024)(128)(2,1)S(1)}, bf16[3072]{0:T(1024)(128)(2,1)}, u32[]{:S(2)}) copy-start(bf16[3072]{0:T(1024)(128)(2,1)} %param.10) | copy-start | bytes 18436
  81.3 15.5 %copy-start.5 = (s32[1024]{0:T(1024)S(1)}, s32[1024]{0:T(1024)}, u32[]{:S(2)}) copy-start(s32[1024]{0:T(1024)} %param.13) | copy-start | bytes 12292
  85.1 7.7 %all-to-all-start = ((f32[4,8,384]{2,1,0:T(8,128)}), f32[4,8,384]{2,1,0:T(8,128)S(1)}, u32[]{:S(2)}, u32[]{:S(2)}) async-start(f32[4,8,384]{2,1,0:T(8,128)} %reshape.27), calls=%async_computation | async-start | bytes 98304 | tf_op jit(solution)/shard_map/all_to_all | solution.py:49
  93.5 31.9 %all-to-all-start.1 = ((f32[4,8,384]{2,0,1:T(4,128)}), f32[4,8,384]{2,0,1:T(4,128)S(1)}, u32[]{:S(2)}, u32[]{:S(2)}) async-start(f32[4,8,384]{2,0,1:T(4,128)} %copy.15), calls=%async_computation.1 | async-start | bytes 98304 | tf_op jit(solution)/shard_map/all_to_all | solution.py:48
  124.8 4.7 %copy-start.3 = (f32[1024]{0:T(1024)}, f32[1024]{0:T(1024)S(1)}, u32[]{:S(2)}) copy-start(f32[1024]{0:T(1024)S(1)} %psum.15) | copy-start | bytes 12292
